TPU v7x, 32 devices: a whole 2x2x4 slice. The times are simulated.
32 devices in a mesh: dp: 4 (over x, core), ctx: 4 (over z), tp: 2 (over y).
Axes of the slice: x: 2, y: 2, z: 4, core: 2. Of those that a mesh axis runs over, the one named last changes fastest.
Arguments:
- tokens: bfloat16 [8192, 2048], P(('dp', 'ctx')), may hold values from -12 to 12, as said below
- gain_one: bfloat16 [2048], P(('dp', 'ctx')), may hold values from 0.099609375 to 1.8984375
- bias_one: bfloat16 [2048], P(('dp', 'ctx')), may hold values from -3 to 3
- w_query: bfloat16 [2048, 2048], P(('dp', 'ctx'), 'tp'), may hold values from -1 to 1, as said below
- w_keyval: bfloat16 [2048, 256], P(('dp', 'ctx')), may hold values from -0.125 to 0.125
- w_out: bfloat16 [2048, 2048], P(('dp', 'ctx'), 'tp'), may hold values from -2 to 2
- gain_two: bfloat16 [2048], P(('dp', 'ctx')), may hold values from 0.099609375 to 1.8984375
- bias_two: bfloat16 [2048], P(('dp', 'ctx')), may hold values from -3 to 3
- w_up: bfloat16 [2048, 8192], P(('dp', 'ctx'), 'tp'), may hold values from -1 to 1, as said below
- w_down: bfloat16 [2048, 8192], P(('dp', 'ctx'), 'tp'), may hold values from -0.0625 to 0.0625
- grad_out: bfloat16 [8192, 2048], P(('dp', 'ctx')), may hold values from -6 to 6
Outputs:
- layer_out: bfloat16 [8192, 2048], P(('dp', 'ctx'))
- input_grad: float32 [8192, 2048], P(('dp', 'ctx'))
- grad_gain_one: float32 [2048], P(('dp', 'ctx'))
- grad_bias_one: float32 [2048], P(('dp', 'ctx'))
- grad_query: float32 [2048, 2048], P(('dp', 'ctx'), 'tp')
- grad_keyval: float32 [2048, 256], P(('dp', 'ctx'))
- grad_out_proj: float32 [2048, 2048], P(('dp', 'ctx'), 'tp')
- grad_gain_two: float32 [2048], P(('dp', 'ctx'))
- grad_bias_two: float32 [2048], P(('dp', 'ctx'))
- grad_up: float32 [2048, 8192], P(('dp', 'ctx'), 'tp')
- grad_down: float32 [2048, 8192], P(('dp', 'ctx'), 'tp')
- rms_values: float32 [3], replicated
Inputs may be any that keep to these rules, and one draw needn't show every extreme that they name: `tokens`: real-valued activations. `w_query`: real-valued projection weights. `w_up`: real-valued projection weights.
All inputs are finite; a program needn't handle non-finite values.
Results may differ from a plain program's by a relative error of at most 0.015.
Values may be sent and summed in bfloat16 or wider, within the bound.
No kernel may reach another device: no remote copies, remote signals or barrier semaphores. Data moves between devices by JAX's collectives and lax.ppermute only.
A program may use at most 256 MiB of HBM per device.

v0:
```python
import jax
import jax.numpy as jnp
from jax import lax
from jax.sharding import PartitionSpec as P

BLOCK = 256
eps_norm = 1e-05
neg_large = -1e30


def layer_norm(values, gain, shift):
    center = values - jnp.mean(values, axis=-1, keepdims=True)
    spread = jnp.mean(center * center, axis=-1, keepdims=True)
    return center * lax.rsqrt(spread + eps_norm) * gain + shift


def gelu_tanh(values):
    return jax.nn.gelu(values, approximate=True)


def last_dot(left, right):
    return lax.dot_general(
        left, right, (((1,), (1,)), ((), ())), preferred_element_type=jnp.float32
    )


def first_dot(left, right):
    return lax.dot_general(
        left, right, (((0,), (0,)), ((), ())), preferred_element_type=jnp.float32
    )


def body(
    tokens, gain_one, bias_one, w_query, w_keyval, w_out, gain_two, bias_two, w_up, w_down, grad_out
):
    rows = tokens.shape[0]
    width = tokens.shape[1]
    head_size = w_keyval.shape[1] // 2
    local_heads = w_query.shape[1] // head_size
    scale = head_size ** (-0.5)
    ctx_index = lax.axis_index("ctx")
    tile_count = ctx_index + 1
    stream = tokens.astype(jnp.float32)
    full_gain_one, full_bias_one, query_full, keyval_full, out_full = (
        lax.all_gather(gain_one, ("dp", "ctx"), axis=0, tiled=True),
        lax.all_gather(bias_one, ("dp", "ctx"), axis=0, tiled=True),
        lax.all_gather(w_query, ("dp", "ctx"), axis=0, tiled=True),
        lax.all_gather(w_keyval, ("dp", "ctx"), axis=0, tiled=True),
        lax.all_gather(w_out, ("dp", "ctx"), axis=0, tiled=True),
    )
    normed_one, norm_one_pull = jax.vjp(
        layer_norm, stream, full_gain_one.astype(jnp.float32), full_bias_one.astype(jnp.float32)
    )
    normed_low = normed_one.astype(jnp.bfloat16)
    queries = jnp.dot(normed_low, query_full, preferred_element_type=jnp.float32).astype(
        jnp.bfloat16
    )
    keyvals = jnp.dot(normed_low, keyval_full, preferred_element_type=jnp.float32).astype(
        jnp.bfloat16
    )
    keyval_all = lax.all_gather(keyvals, "ctx", axis=0, tiled=True)
    keys_all = keyval_all[:, :head_size]
    values_all = keyval_all[:, head_size:]
    query_heads = queries.reshape(rows, local_heads, head_size)
    query_block = (ctx_index * rows + jnp.arange(rows, dtype=jnp.int32)) // BLOCK

    def tile_scores(tile):
        start = tile * rows
        key_tile = lax.dynamic_slice_in_dim(keys_all, start, rows, 0)
        value_tile = lax.dynamic_slice_in_dim(values_all, start, rows, 0)
        scores = (
            jnp.einsum("qhd,kd->hqk", query_heads, key_tile, preferred_element_type=jnp.float32)
            * scale
        )
        key_block = (start + jnp.arange(rows, dtype=jnp.int32)) // BLOCK
        allowed = (key_block[None, :] <= query_block[:, None])[None]
        return (scores, allowed, key_tile, value_tile)

    def max_step(tile, carry):
        run_max, run_sum = carry
        scores, allowed, key_tile, value_tile = tile_scores(tile)
        masked = jnp.where(allowed, scores, neg_large)
        new_max = jnp.maximum(run_max, jnp.max(masked, axis=-1))
        run_sum = run_sum * jnp.exp(run_max - new_max) + jnp.sum(
            jnp.exp(masked - new_max[..., None]), axis=-1
        )
        return (new_max, run_sum)

    start_max = jnp.full((local_heads, rows), neg_large, jnp.float32)
    start_sum = jnp.zeros((local_heads, rows), jnp.float32)
    row_max, row_sum = lax.fori_loop(0, tile_count, max_step, (start_max, start_sum))
    log_total = row_max + jnp.log(row_sum)

    def value_step(tile, accum):
        scores, allowed, key_tile, value_tile = tile_scores(tile)
        probs = jnp.where(allowed, jnp.exp(scores - log_total[..., None]), 0.0)
        return accum + jnp.einsum(
            "hqk,kd->qhd",
            probs.astype(jnp.bfloat16),
            value_tile,
            preferred_element_type=jnp.float32,
        )

    attn_accum = lax.fori_loop(
        0, tile_count, value_step, jnp.zeros((rows, local_heads, head_size), jnp.float32)
    )
    attn_low = attn_accum.reshape(rows, local_heads * head_size).astype(jnp.bfloat16)
    branch_attn = lax.psum(last_dot(attn_low, out_full).astype(jnp.bfloat16), "tp").astype(
        jnp.float32
    )
    hidden = stream + branch_attn
    full_gain_two, full_bias_two, up_full, down_full = (
        lax.all_gather(gain_two, ("dp", "ctx"), axis=0, tiled=True),
        lax.all_gather(bias_two, ("dp", "ctx"), axis=0, tiled=True),
        lax.all_gather(w_up, ("dp", "ctx"), axis=0, tiled=True),
        lax.all_gather(w_down, ("dp", "ctx"), axis=0, tiled=True),
    )
    normed_two, norm_two_pull = jax.vjp(
        layer_norm, hidden, full_gain_two.astype(jnp.float32), full_bias_two.astype(jnp.float32)
    )
    normed_two_low = normed_two.astype(jnp.bfloat16)
    pre_act = jnp.dot(normed_two_low, up_full, preferred_element_type=jnp.float32)
    act_value, gelu_pull = jax.vjp(gelu_tanh, pre_act)
    act_low = act_value.astype(jnp.bfloat16)
    branch_mlp = lax.psum(last_dot(act_low, down_full).astype(jnp.bfloat16), "tp").astype(
        jnp.float32
    )
    result = hidden + branch_mlp
    square_sums = lax.psum(
        jnp.stack(
            [
                jnp.sum(result * result),
                jnp.sum(branch_attn * branch_attn),
                jnp.sum(branch_mlp * branch_mlp),
            ]
        ),
        ("dp", "ctx"),
    )
    entry_count = rows * lax.axis_size("dp") * lax.axis_size("ctx") * width
    rms_values = jnp.sqrt(square_sums / entry_count)
    grad_result = grad_out.astype(jnp.float32)
    grad_act = jnp.dot(grad_out, down_full, preferred_element_type=jnp.float32)
    grad_down = first_dot(grad_out, act_low)
    grad_pre_low = gelu_pull(grad_act)[0].astype(jnp.bfloat16)
    grad_up = first_dot(normed_two_low, grad_pre_low)
    grad_normed_two = lax.psum(last_dot(grad_pre_low, up_full).astype(jnp.bfloat16), "tp").astype(
        jnp.float32
    )
    grad_hidden_norm, grad_gain_two, grad_bias_two = norm_two_pull(grad_normed_two)
    grad_hidden = grad_result + grad_hidden_norm
    grad_gain_two, grad_bias_two, grad_up, grad_down = (
        lax.psum_scatter(grad_gain_two, ("dp", "ctx"), scatter_dimension=0, tiled=True),
        lax.psum_scatter(grad_bias_two, ("dp", "ctx"), scatter_dimension=0, tiled=True),
        lax.psum_scatter(grad_up, ("dp", "ctx"), scatter_dimension=0, tiled=True),
        lax.psum_scatter(grad_down, ("dp", "ctx"), scatter_dimension=0, tiled=True),
    )
    grad_branch_low = grad_hidden.astype(jnp.bfloat16)
    grad_out_proj = first_dot(grad_branch_low, attn_low)
    grad_heads_low = jnp.dot(grad_branch_low, out_full, preferred_element_type=jnp.float32).astype(
        jnp.bfloat16
    )
    grad_heads = grad_heads_low.reshape(rows, local_heads, head_size)
    row_delta = jnp.sum(grad_heads.astype(jnp.float32) * attn_accum, axis=-1).T

    def back_step(tile, carry):
        grad_query_acc, grad_keyval_all = carry
        scores, allowed, key_tile, value_tile = tile_scores(tile)
        probs = jnp.where(allowed, jnp.exp(scores - log_total[..., None]), 0.0)
        grad_probs = jnp.einsum(
            "qhd,kd->hqk", grad_heads, value_tile, preferred_element_type=jnp.float32
        )
        grad_scores = (probs * (grad_probs - row_delta[..., None])).astype(jnp.bfloat16)
        grad_query_acc = grad_query_acc + jnp.einsum(
            "hqk,kd->qhd", grad_scores, key_tile, preferred_element_type=jnp.float32
        )
        grad_key_tile = (
            jnp.einsum("hqk,qhd->kd", grad_scores, query_heads, preferred_element_type=jnp.float32)
            * scale
        )
        grad_value_tile = jnp.einsum(
            "hqk,qhd->kd",
            probs.astype(jnp.bfloat16),
            grad_heads,
            preferred_element_type=jnp.float32,
        )
        grad_keyval_all = lax.dynamic_update_slice_in_dim(
            grad_keyval_all,
            jnp.concatenate([grad_key_tile, grad_value_tile], axis=1),
            tile * rows,
            0,
        )
        return (grad_query_acc, grad_keyval_all)

    start_query = jnp.zeros((rows, local_heads, head_size), jnp.float32)
    start_keyval = jnp.zeros(keyval_all.shape, jnp.float32)
    grad_query_acc, grad_keyval_all = lax.fori_loop(
        0, tile_count, back_step, (start_query, start_keyval)
    )
    grad_query_low = (
        (grad_query_acc * scale).reshape(rows, local_heads * head_size).astype(jnp.bfloat16)
    )
    grad_keyval_mine = lax.psum_scatter(
        grad_keyval_all.astype(jnp.bfloat16), "ctx", scatter_dimension=0, tiled=True
    )
    grad_normed_query = last_dot(grad_query_low, query_full)
    grad_normed_part, grad_keyval_sum = (
        lax.psum(grad_normed_query.astype(jnp.bfloat16), "tp").astype(jnp.float32),
        lax.psum(grad_keyval_mine, "tp").astype(jnp.float32),
    )
    grad_keyval_low = grad_keyval_sum.astype(jnp.bfloat16)
    grad_normed_one = grad_normed_part + last_dot(grad_keyval_low, keyval_full)
    grad_query = first_dot(normed_low, grad_query_low)
    grad_keyval = first_dot(normed_low, grad_keyval_low)
    grad_stream_norm, grad_gain_one, grad_bias_one = norm_one_pull(grad_normed_one)
    input_grad = grad_hidden + grad_stream_norm
    grad_gain_one, grad_bias_one, grad_query, grad_keyval, grad_out_proj = (
        lax.psum_scatter(grad_gain_one, ("dp", "ctx"), scatter_dimension=0, tiled=True),
        lax.psum_scatter(grad_bias_one, ("dp", "ctx"), scatter_dimension=0, tiled=True),
        lax.psum_scatter(grad_query, ("dp", "ctx"), scatter_dimension=0, tiled=True),
        lax.psum_scatter(grad_keyval, ("dp", "ctx"), scatter_dimension=0, tiled=True),
        lax.psum_scatter(grad_out_proj, ("dp", "ctx"), scatter_dimension=0, tiled=True),
    )
    return (
        result.astype(jnp.bfloat16),
        input_grad,
        grad_gain_one,
        grad_bias_one,
        grad_query,
        grad_keyval,
        grad_out_proj,
        grad_gain_two,
        grad_bias_two,
        grad_up,
        grad_down,
        rms_values,
    )


def solution(mesh):
    return jax.shard_map(
        body,
        mesh=mesh,
        in_specs=(
            P(("dp", "ctx"), None),
            P(("dp", "ctx")),
            P(("dp", "ctx")),
            P(("dp", "ctx"), "tp"),
            P(("dp", "ctx"), None),
            P(("dp", "ctx"), "tp"),
            P(("dp", "ctx")),
            P(("dp", "ctx")),
            P(("dp", "ctx"), "tp"),
            P(("dp", "ctx"), "tp"),
            P(("dp", "ctx"), None),
        ),
        out_specs=(
            P(("dp", "ctx"), None),
            P(("dp", "ctx"), None),
            P(("dp", "ctx")),
            P(("dp", "ctx")),
            P(("dp", "ctx"), "tp"),
            P(("dp", "ctx"), None),
            P(("dp", "ctx"), "tp"),
            P(("dp", "ctx")),
            P(("dp", "ctx")),
            P(("dp", "ctx"), "tp"),
            P(("dp", "ctx"), "tp"),
            P(),
        ),
        check_vma=False,
    )
```

profile of v0, /device:TPU:0, one launch (start us, length us, event | category | flops | bytes accessed | tf_op | source)
XLA Modules:
  0.0 1833.9 jit_solution(2962413026030763452)
XLA Ops:
  8.0 33.8 %all-gather.1 = bf16[16,1,128]{2,1,0:T(2,128)(2,1)S(1)} all-gather(bf16[1,1,128]{2,1,0:T(2,128)(2,1)} %bitcast.192), channel_id=1, replica_groups=mesh['dp'=4,'ctx'=4,'tp'=2] {'dp','ctx'}, dimensions={0}, use_global_device_ids=true | all-gather | bytes 4352 | tf_op jit(solution)/shard_map/all_gather | solution.py:46
  41.8 28.4 %all-gather = bf16[16,1,128]{2,1,0:T(2,128)(2,1)S(1)} all-gather(bf16[1,1,128]{2,1,0:T(2,128)(2,1)} %bitcast.193), channel_id=1, replica_groups=mesh['dp'=4,'ctx'=4,'tp'=2] {'dp','ctx'}, dimensions={0}, use_global_device_ids=true | all-gather | bytes 4352 | tf_op jit(solution)/shard_map/all_gather | solution.py:45
  82.6 25.4 %all-gather.13.cloned.1.call-done = bf16[2048,256]{1,0:T(8,128)(2,1)} async-done(((bf16[512,256]{1,0:T(8,128)(2,1)}), bf16[2048,256]{1,0:T(8,128)(2,1)}) %all-gather.13.cloned.1.call-update) | async-done | bytes 1048592 | tf_op jit(solution)/shard_map/all_gather | solution.py:61
  110.3 50.2 %all-gather.15.cloned.1.call-done = bf16[2048,1024]{1,0:T(8,128)(2,1)} async-done(((bf16[128,1024]{1,0:T(8,128)(2,1)}), bf16[2048,1024]{1,0:T(8,128)(2,1)}) %all-gather.15.cloned.1.call-update) | async-done | bytes 4194320 | tf_op jit(solution)/shard_map/all_gather | solution.py:47
  173.2 5.8 while.44
  180.7 31.1 %all-gather.17.cloned.1.call-done = bf16[2048,1024]{1,0:T(8,128)(2,1)} async-done(((bf16[128,1024]{1,0:T(8,128)(2,1)}), bf16[2048,1024]{1,0:T(8,128)(2,1)}) %all-gather.17.cloned.1.call-update) | async-done | bytes 4194320 | tf_op jit(solution)/shard_map/all_gather | solution.py:49
  211.9 5.9 convolution_convert_fusion.1
  219.2 29.9 %all-gather.3 = bf16[16,1,128]{2,1,0:T(2,128)(2,1)S(1)} all-gather(bf16[1,1,128]{2,1,0:T(2,128)(2,1)S(1)} %bitcast.194), channel_id=1, replica_groups=mesh['dp'=4,'ctx'=4,'tp'=2] {'dp','ctx'}, dimensions={0}, use_global_device_ids=true | all-gather | bytes 4352 | tf_op jit(solution)/shard_map/all_gather | solution.py:114
  249.1 29.0 %all-gather.2 = bf16[16,1,128]{2,1,0:T(2,128)(2,1)S(1)} all-gather(bf16[1,1,128]{2,1,0:T(2,128)(2,1)S(1)} %bitcast.195), channel_id=1, replica_groups=mesh['dp'=4,'ctx'=4,'tp'=2] {'dp','ctx'}, dimensions={0}, use_global_device_ids=true | all-gather | bytes 4352 | tf_op jit(solution)/shard_map/all_gather | solution.py:113
  282.7 125.9 %all-gather.21.cloned.1.call-done = bf16[2048,4096]{1,0:T(8,128)(2,1)} async-done(((bf16[128,4096]{1,0:T(8,128)(2,1)}), bf16[2048,4096]{1,0:T(8,128)(2,1)}) %all-gather.21.cloned.1.call-update) | async-done | bytes 16777232 | tf_op jit(solution)/shard_map/all_gather | solution.py:116
  408.6 14.9 fusion.111
  423.5 112.6 %all-gather.19.cloned.1.call-done = bf16[2048,4096]{1,0:T(8,128)(2,1)} async-done(((bf16[128,4096]{1,0:T(8,128)(2,1)}), bf16[2048,4096]{1,0:T(8,128)(2,1)}) %all-gather.19.cloned.1.call-update) | async-done | bytes 16777232 | tf_op jit(solution)/shard_map/all_gather | solution.py:115
  536.1 21.0 %fusion.81 = (bf16[512,4096]{1,0:T(8,128)(2,1)S(1)}, f32[512,4096]{1,0:T(8,128)}) fusion(f32[512,4096]{1,0:T(8,128)} %fusion.111, bf16[2048,4096]{1,0:T(8,128)(2,1)} %all-gather.19.cloned.1.call-done, bf16[512,2048]{1,0:T(8,128)(2,1)} %all-reduce.11.cloned.1.call-done, bf16[512,2048]{1,0:T(8,128)(2,1)S(1)} %copy-done, f32[2048]{0:T(1024)S(1)} %bitcast.190, ...), kind=kOutput, calls=%fused_computation.119 | convolution fusion | flops 8640266240 | bytes 41963520 | tf_op jit(solution)/shard_map/dot_general | solution.py:122
  557.1 18.5 %convolution_convert_fusion.3 = bf16[512,2048]{1,0:T(8,128)(2,1)} fusion(bf16[2048,4096]{1,0:T(8,128)(2,1)} %all-gather.21.cloned.1.call-done, f32[512,4096]{1,0:T(8,128)} %get-tuple-element.583), kind=kOutput, calls=%fused_computation.160 | convolution fusion | flops 8609857536 | bytes 27262976 | tf_op jit(solution)/shard_map/dot_general | solution.py:22
  575.6 13.4 convolution_convert_fusion.2
  591.0 104.7 %all-reduce.15.cloned.1.call-done = (bf16[512,2048]{1,0:T(8,128)(2,1)}, bf16[512,2048]{1,0:T(8,128)(2,1)}) async-done(((bf16[512,2048]{1,0:T(8,128)(2,1)}, bf16[512,2048]{1,0:T(8,128)(2,1)}), (bf16[512,2048]{1,0:T(8,128)(2,1)}, bf16[512,2048]{1,0:T(8,128)(2,1)})) %all-reduce.15.cloned.1.call-update) | async-done | bytes 4194320 | tf_op jit(solution)/shard_map/psum | solution.py:125
  695.6 7.0 fusion.98
  719.7 12.7 while.45
  734.3 5.9 convolution_convert_fusion
  740.2 56.9 %reduce-scatter.7.cloned.1.call-done = bf16[512,256]{0,1:T(8,128)(2,1)} async-done(((bf16[2048,256]{0,1:T(8,128)(2,1)}), bf16[512,256]{0,1:T(8,128)(2,1)}) %reduce-scatter.7.cloned.1.call-update) | async-done | bytes 262160 | tf_op jit(solution)/shard_map/reduce_scatter | solution.py:202
  797.2 21.1 %convolution_bitcast_fusion.1 = f32[2048,4096]{0,1:T(8,128)} fusion(bf16[512,2048]{1,0:T(8,128)(2,1)} %param.27, f32[512,4096]{1,0:T(8,128)} %get-tuple-element.583), kind=kOutput, calls=%fused_computation.110 | convolution fusion | flops 8608808960 | bytes 44040192 | tf_op jit(solution)/shard_map/dot_general | solution.py:28
  818.4 49.2 %all-reduce.13.cloned.1.call-done = (bf16[512,2048]{1,0:T(8,128)(2,1)}, bf16[512,256]{0,1:T(8,128)(2,1)}) async-done(((bf16[512,2048]{1,0:T(8,128)(2,1)}, bf16[512,256]{0,1:T(8,128)(2,1)}), (bf16[512,2048]{1,0:T(8,128)(2,1)}, bf16[512,256]{0,1:T(8,128)(2,1)})) %all-reduce.13.cloned.1.call-update) | async-done | bytes 2359312 | tf_op jit(solution)/shard_map/psum | solution.py:207
  871.3 7.6 fusion.112
  880.4 8.9 fusion.114
  890.0 25.4 %fusion.106 = f32[2048,4096]{1,0:T(8,128)} fusion(bf16[512,4096]{1,0:T(8,128)(2,1)} %copy-done.33, bf16[512,2048]{1,0:T(8,128)(2,1)} %all-reduce.11.cloned.1.call-done, bf16[512,2048]{1,0:T(8,128)(2,1)S(1)} %copy-done, f32[2048]{0:T(1024)S(1)} %bitcast.191, f32[2048]{0:T(1024)S(1)} %bitcast.187, f32[512]{0:T(512)S(1)} %fusion.104, ...), kind=kOutput, calls=%fused_computation.183 | convolution fusion | flops 8598323200 | bytes 41963520 | tf_op jit(solution)/shard_map/dot_general | solution.py:28
  926.7 66.4 %all-reduce.4 = (f32[2048]{0:T(1024)S(1)}, f32[2048]{0:T(1024)S(1)}, f32[2048]{0:T(1024)S(1)}, f32[2048]{0:T(1024)S(1)}, f32[3]{0:T(128)S(1)}) all-reduce(f32[2048]{0:T(1024)S(1)} %get-tuple-element.498, f32[2048]{0:T(1024)S(1)} %get-tuple-element.503, ...), channel_id=3, replica_groups=mesh['dp'=4,'ctx'=4,'tp'=2] {'dp','ctx'}, use_global_device_ids=true, to_apply=%region_24.25.clone | all-reduce | flops 8195 | bytes 65560
  996.0 6.7 add_add_fusion.2
  1002.7 203.6 %reduce-scatter.17.cloned.1.call-done = f32[128,4096]{0,1:T(8,128)} async-done(((f32[2048,4096]{0,1:T(8,128)}), f32[128,4096]{0,1:T(8,128)}) %reduce-scatter.17.cloned.1.call-update) | async-done | bytes 2097168 | tf_op jit(solution)/shard_map/reduce_scatter | solution.py:155
  1209.1 61.9 %reduce-scatter.11.cloned.1.call-done = f32[128,256]{1,0:T(8,128)} async-done(((f32[2048,256]{1,0:T(8,128)}), f32[128,256]{1,0:T(8,128)}) %reduce-scatter.11.cloned.1.call-update) | async-done | bytes 131088 | tf_op jit(solution)/shard_map/reduce_scatter | solution.py:220
  1271.0 108.8 %reduce-scatter.9.cloned.1.call-done = f32[128,1024]{1,0:T(8,128)} async-done(((f32[2048,1024]{1,0:T(8,128)}), f32[128,1024]{1,0:T(8,128)}) %reduce-scatter.9.cloned.1.call-update) | async-done | bytes 524304 | tf_op jit(solution)/shard_map/reduce_scatter | solution.py:219
  1379.8 109.4 %reduce-scatter.13.cloned.1.call-done = f32[128,1024]{1,0:T(8,128)} async-done(((f32[2048,1024]{1,0:T(8,128)}), f32[128,1024]{1,0:T(8,128)}) %reduce-scatter.13.cloned.1.call-update) | async-done | bytes 524304 | tf_op jit(solution)/shard_map/reduce_scatter | solution.py:221
  1489.3 337.7 %reduce-scatter.15.cloned.1.call-done = f32[128,4096]{1,0:T(8,128)} async-done(((f32[2048,4096]{1,0:T(8,128)}), f32[128,4096]{1,0:T(8,128)}) %reduce-scatter.15.cloned.1.call-update) | async-done | bytes 2097168 | tf_op jit(solution)/shard_map/reduce_scatter | solution.py:154
  (166 shorter events, 101.3 us)
Async XLA Ops:
  7.2 68.4 %copy-start = (bf16[512,2048]{1,0:T(8,128)(2,1)S(1)}, bf16[512,2048]{1,0:T(8,128)(2,1)}, u32[]{:S(2)}) copy-start(bf16[512,2048]{1,0:T(8,128)(2,1)} %param.17) | copy-start | bytes 6291460
  7.2 70.6 %all-gather.11.cloned.1.call-start = ((), (), s32[]{:S(2)}) async-start(), calls=%async_computation.6 | async-start | bytes 1114112 | tf_op jit(solution)/shard_map/all_gather | solution.py:48
  7.9 100.2 %all-gather.13.cloned.1.call-start = ((), (), s32[]{:S(2)}) async-start(), calls=%async_computation.7 | async-start | bytes 1310720 | tf_op jit(solution)/shard_map/all_gather | solution.py:61
  70.2 4.8 copy-start.15
  81.1 79.5 %all-gather.15.cloned.1.call-start = ((), (), s32[]{:S(2)}) async-start(), calls=%async_computation.8 | async-start | bytes 4456448 | tf_op jit(solution)/shard_map/all_gather | solution.py:47
  81.8 130.1 %all-gather.17.cloned.1.call-start = ((), (), s32[]{:S(2)}) async-start(), calls=%async_computation.9 | async-start | bytes 4456448 | tf_op jit(solution)/shard_map/all_gather | solution.py:49
  82.4 197.0 %all-reduce.11.cloned.1.call-start = ((), (), s32[]{:S(2)}) async-start(), calls=%async_computation.10 | async-start | bytes 4194304 | tf_op jit(solution)/shard_map/psum | solution.py:108
  180.7 37.0 %copy-start.13 = (bf16[512,8,128]{0,2,1:T(8,128)(2,1)}, bf16[512,8,128]{0,2,1:T(8,128)(2,1)S(1)}, u32[]{:S(2)}) copy-start(bf16[512,8,128]{0,2,1:T(8,128)(2,1)S(1)} %convert_element_type.113) | copy-start | bytes 3145732
  217.8 31.4 %copy-start.30 = (bf16[128]{0:T(256)(128)(2,1)S(1)}, bf16[128]{0:T(256)(128)(2,1)}, u32[]{:S(2)}) copy-start(bf16[128]{0:T(256)(128)(2,1)} %param.23) | copy-start | bytes 772
  217.8 190.8 %all-gather.21.cloned.1.call-start = ((), (), s32[]{:S(2)}) async-start(), calls=%async_computation.12 | async-start | bytes 17825792 | tf_op jit(solution)/shard_map/all_gather | solution.py:116
  218.4 317.8 %all-gather.19.cloned.1.call-start = ((), (), s32[]{:S(2)}) async-start(), calls=%async_computation.11 | async-start | bytes 17825792 | tf_op jit(solution)/shard_map/all_gather | solution.py:115
  219.1 476.5 %all-reduce.15.cloned.1.call-start = ((), (), s32[]{:S(2)}) async-start(), calls=%async_computation.20 | async-start | bytes 8388608 | tf_op jit(solution)/shard_map/psum | solution.py:125
  249.1 287.0 %copy-start.27 = (f32[16,1,128]{2,1,0:T(1,128)}, f32[16,1,128]{2,1,0:T(1,128)S(1)}, u32[]{:S(2)}) copy-start(f32[16,1,128]{2,1,0:T(1,128)S(1)} %convert_element_type.139) | copy-start | bytes 24580
  557.1 18.5 %copy-start.33 = (bf16[512,4096]{1,0:T(8,128)(2,1)}, bf16[512,4096]{1,0:T(8,128)(2,1)S(1)}, u32[]{:S(2)}) copy-start(bf16[512,4096]{1,0:T(8,128)(2,1)S(1)} %get-tuple-element.582) | copy-start | bytes 12582916
  589.1 208.1 %reduce-scatter.7.cloned.1.call-start = ((), (), s32[]{:S(2)}) async-start(), calls=%async_computation.13 | async-start | bytes 1310720 | tf_op jit(solution)/shard_map/reduce_scatter | solution.py:202
  695.6 7.0 copy-start.6
  695.6 7.0 copy-start.8
  704.7 4.4 copy-start.31
  732.4 135.2 %all-reduce.13.cloned.1.call-start = ((), (), s32[]{:S(2)}) async-start(), calls=%async_computation.19 | async-start | bytes 4718592 | tf_op jit(solution)/shard_map/psum | solution.py:207
  797.2 409.1 %reduce-scatter.17.cloned.1.call-start = ((), (), s32[]{:S(2)}) async-start(), calls=%async_computation.18 | async-start | bytes 35651584 | tf_op jit(solution)/shard_map/reduce_scatter | solution.py:155
  818.3 452.7 %reduce-scatter.11.cloned.1.call-start = ((), (), s32[]{:S(2)}) async-start(), calls=%async_computation.15 | async-start | bytes 2228224 | tf_op jit(solution)/shard_map/reduce_scatter | solution.py:220
  871.3 508.6 %reduce-scatter.9.cloned.1.call-start = ((), (), s32[]{:S(2)}) async-start(), calls=%async_computation.14 | async-start | bytes 8912896 | tf_op jit(solution)/shard_map/reduce_scatter | solution.py:219
  878.9 610.3 %reduce-scatter.13.cloned.1.call-start = ((), (), s32[]{:S(2)}) async-start(), calls=%async_computation.16 | async-start | bytes 8912896 | tf_op jit(solution)/shard_map/reduce_scatter | solution.py:221
  889.3 937.6 %reduce-scatter.15.cloned.1.call-start = ((), (), s32[]{:S(2)}) async-start(), calls=%async_computation.17 | async-start | bytes 35651584 | tf_op jit(solution)/shard_map/reduce_scatter | solution.py:154
  915.4 3.9 copy-start.11
  915.4 3.9 copy-start.12
  915.4 3.9 copy-start.16
  915.4 3.9 copy-start.18
  919.4 5.3 copy-start.20
  922.7 4.0 copy-start.21
  922.7 4.0 copy-start.22
  922.7 73.3 %copy-start.24 = (f32[512]{0:T(512)S(1)}, f32[512]{0:T(512)}, u32[]{:S(2)}) copy-start(f32[512]{0:T(512)} %copy-done.23) | copy-start | bytes 6148
  (17 other events, 31.8 us)
Sparse Core Ops, SparseCore 0:
  10.2 40.6 all-gather.10
  81.2 26.8 all-gather.12
  110.3 50.1 all-gather.14
  162.6 49.2 all-gather.16
  217.9 61.4 all-reduce.10
  281.7 126.8 all-gather.20
  411.1 125.0 all-gather.18
  589.2 106.3 all-reduce.14
  732.5 64.5 reduce-scatter.6
  800.1 67.4 all-reduce.12
  871.8 334.3 reduce-scatter.16
  1210.4 60.5 reduce-scatter.10
  1276.2 103.5 reduce-scatter.8
  1384.9 104.3 reduce-scatter.12
  1494.5 332.3 reduce-scatter.14
where the time goes:
time: 1840 us; the launch traced here: 1830 us
  waiting for transfers between devices  1380 us (75%)
  blocking collectives  188 us (10%)
  matrix products  181 us (10%)
  other arithmetic  39.6 us (2%)
  local copies, waits for them, and re-layouts  27.3 us (1%)
    reduce_scatter x1, waiting for transfers between devices, body(): lax.psum_scatter(grad_up, ('dp', 'ctx'), scatter_dimension=0, tiled=True)  338 us
    reduce_scatter x1, waiting for transfers between devices, body(): lax.psum_scatter(grad_down, ('dp', 'ctx'), scatter_dimension=0, tiled=True)  204 us
    all_gather x1, waiting for transfers between devices, body(): lax.all_gather(w_down, ('dp', 'ctx'), axis=0, tiled=True)  126 us
    all_gather x1, waiting for transfers between devices, body(): lax.all_gather(w_up, ('dp', 'ctx'), axis=0, tiled=True)  113 us
    reduce_scatter x1, waiting for transfers between devices, body(): lax.psum_scatter(grad_out_proj, ('dp', 'ctx'), scatter_dimension=0, tiled...  109 us
    reduce_scatter x1, waiting for transfers between devices, body(): lax.psum_scatter(grad_query, ('dp', 'ctx'), scatter_dimension=0, tiled=True)  109 us
    psum x1, waiting for transfers between devices, body(): lax.psum(last_dot(act_low, down_full).astype(jnp.bfloat16), 'tp')  105 us
    dot_general x5, matrix products, first_dot(): lax.dot_general(left, right, (((0,), (0,)), ((), ())), preferred_element_...  66.7 us
  transfers between devices with their start and end apart: 15, of which 14 were waited for; matrix products, arithmetic and copies ran while one was open for 8% of the time, Pallas kernels for 0%

commit v1 on v0

--- a/solution.py
+++ b/solution.py
@@ -6,6 +6,24 @@
 BLOCK = 256
 eps_norm = 1e-05
 neg_large = -1e30
+
+
+def ring_gather(value, axis, dim):
+    ways, here, lap = (lax.axis_size(axis), lax.axis_index(axis), value.shape[dim])
+    shape = [n * ways if d == dim else n for d, n in enumerate(value.shape)]
+    full = lax.dynamic_update_slice_in_dim(
+        jnp.zeros(shape, value.dtype), value, here * lap, axis=dim
+    )
+    going_up = going_down = value
+    for far in range(1, ways // 2 + 1):
+        going_up = lax.ppermute(going_up, axis, [(d, (d + 1) % ways) for d in range(ways)])
+        full = lax.dynamic_update_slice_in_dim(full, going_up, (here - far) % ways * lap, axis=dim)
+        if 2 * far < ways:
+            going_down = lax.ppermute(going_down, axis, [(d, (d - 1) % ways) for d in range(ways)])
+            full = lax.dynamic_update_slice_in_dim(
+                full, going_down, (here + far) % ways * lap, axis=dim
+            )
+    return full
 
 
 def layer_norm(values, gain, shift):
@@ -112,7 +130,7 @@
     full_gain_two, full_bias_two, up_full, down_full = (
         lax.all_gather(gain_two, ("dp", "ctx"), axis=0, tiled=True),
         lax.all_gather(bias_two, ("dp", "ctx"), axis=0, tiled=True),
-        lax.all_gather(w_up, ("dp", "ctx"), axis=0, tiled=True),
+        ring_gather(w_up, ("dp", "ctx"), 0),
         lax.all_gather(w_down, ("dp", "ctx"), axis=0, tiled=True),
     )
     normed_two, norm_two_pull = jax.vjp(

time: 1840 us -> 2020 us (1.098)
  blocking collectives: 188 us -> 264 us
  waiting for transfers between devices: 1380 us -> 1430 us
  local copies, waits for them, and re-layouts: 27.3 us -> 58.7 us
  starting transfers between devices: 1.06 us -> 30.1 us
    ppermute x0 -> x15, waiting for transfers between devices: none -> 285 us  [the longest x7 164 us: ring_gather(): lax.ppermute(going_down, axis, [(d, (d - 1) % ways) for d in range(ways)])]
    all_gather x1, waiting for transfers between devices: 126 us -> 0.02 us  [body(): lax.all_gather(w_down, ('dp', 'ctx'), axis=0, tiled=True)]
    all_gather x1 -> x0, waiting for transfers between devices: 113 us -> none  [body(): lax.all_gather(w_up, ('dp', 'ctx'), axis=0, tiled=True)]
    all_gather x1, blocking collectives: 29.9 us -> 107 us  [body(): lax.all_gather(bias_two, ('dp', 'ctx'), axis=0, tiled=True)]
    ppermute x0 -> x15, starting transfers between devices: none -> 29.3 us  [the longest x7 19 us: ring_gather(): lax.ppermute(going_down, axis, [(d, (d - 1) % ways) for d in range(ways)])]
    dynamic_update_slice x0 -> x16, local copies, waits for them, and re-layouts: none -> 24.5 us  [the longest x8 13.5 us: ring_gather(): lax.dynamic_update_slice_in_dim(full, going_up, (here - far) % ways * lap...]
  transfers between devices with their start and end apart: 15 -> 29, of which waited for: 14 -> 24; matrix products, arithmetic and copies ran while one was open for 8% -> 8% of each run, Pallas kernels for 0% -> 0%
where the time goes in v1:
time: 2020 us
  waiting for transfers between devices  1430 us (71%)
  blocking collectives  264 us (13%)
  matrix products  181 us (9%)
  local copies, waits for them, and re-layouts  58.7 us (3%)
  other arithmetic  39.6 us (2%)
  starting transfers between devices  30.1 us (1%)
    reduce_scatter x1, waiting for transfers between devices, body(): lax.psum_scatter(grad_up, ('dp', 'ctx'), scatter_dimension=0, tiled=True)  338 us
    reduce_scatter x1, waiting for transfers between devices, body(): lax.psum_scatter(grad_down, ('dp', 'ctx'), scatter_dimension=0, tiled=True)  204 us
    ppermute x7, waiting for transfers between devices, ring_gather(): lax.ppermute(going_down, axis, [(d, (d - 1) % ways) for d in range(ways)])  164 us
    ppermute x8, waiting for transfers between devices, ring_gather(): lax.ppermute(going_up, axis, [(d, (d + 1) % ways) for d in range(ways)])  121 us
    reduce_scatter x1, waiting for transfers between devices, body(): lax.psum_scatter(grad_out_proj, ('dp', 'ctx'), scatter_dimension=0, tiled...  110 us
    reduce_scatter x1, waiting for transfers between devices, body(): lax.psum_scatter(grad_query, ('dp', 'ctx'), scatter_dimension=0, tiled=True)  109 us
    psum x1, waiting for transfers between devices, body(): lax.psum(last_dot(act_low, down_full).astype(jnp.bfloat16), 'tp')  107 us
    all_gather x1, blocking collectives, body(): lax.all_gather(bias_two, ('dp', 'ctx'), axis=0, tiled=True)  107 us
  transfers between devices with their start and end apart: 29, of which 24 were waited for; matrix products, arithmetic and copies ran while one was open for 8% of the time, Pallas kernels for 0%

profile of v1, /device:TPU:0, one launch (start us, length us, event | category | flops | bytes accessed | tf_op | source)
XLA Modules:
  0.0 2018.0 jit_solution(17091627043761234696)
XLA Ops:
  8.0 33.8 %all-gather.1 = bf16[16,1,128]{2,1,0:T(2,128)(2,1)S(1)} all-gather(bf16[1,1,128]{2,1,0:T(2,128)(2,1)} %bitcast.192), channel_id=1, replica_groups=mesh['dp'=4,'ctx'=4,'tp'=2] {'dp','ctx'}, dimensions={0}, use_global_device_ids=true | all-gather | bytes 4352 | tf_op jit(solution)/shard_map/all_gather | solution.py:64
  41.8 28.4 %all-gather = bf16[16,1,128]{2,1,0:T(2,128)(2,1)S(1)} all-gather(bf16[1,1,128]{2,1,0:T(2,128)(2,1)} %bitcast.193), channel_id=1, replica_groups=mesh['dp'=4,'ctx'=4,'tp'=2] {'dp','ctx'}, dimensions={0}, use_global_device_ids=true | all-gather | bytes 4352 | tf_op jit(solution)/shard_map/all_gather | solution.py:63
  82.7 25.4 %all-gather.12.cloned.1.call-done = bf16[2048,256]{1,0:T(8,128)(2,1)} async-done(((bf16[512,256]{1,0:T(8,128)(2,1)}), bf16[2048,256]{1,0:T(8,128)(2,1)}) %all-gather.12.cloned.1.call-update) | async-done | bytes 1048592 | tf_op jit(solution)/shard_map/all_gather | solution.py:79
  110.4 50.2 %all-gather.14.cloned.1.call-done = bf16[2048,1024]{1,0:T(8,128)(2,1)} async-done(((bf16[128,1024]{1,0:T(8,128)(2,1)}), bf16[2048,1024]{1,0:T(8,128)(2,1)}) %all-gather.14.cloned.1.call-update) | async-done | bytes 4194320 | tf_op jit(solution)/shard_map/all_gather | solution.py:65
  181.4 30.3 %all-gather.16.cloned.1.call-done = bf16[2048,1024]{1,0:T(8,128)(2,1)} async-done(((bf16[128,1024]{1,0:T(8,128)(2,1)}), bf16[2048,1024]{1,0:T(8,128)(2,1)}) %all-gather.16.cloned.1.call-update) | async-done | bytes 4194320 | tf_op jit(solution)/shard_map/all_gather | solution.py:67
  222.8 23.9 %collective-permute-done = bf16[128,4096]{1,0:T(8,128)(2,1)S(1)} collective-permute-done((bf16[128,4096]{1,0:T(8,128)(2,1)}, bf16[128,4096]{1,0:T(8,128)(2,1)S(1)}, u32[]{:S(2)}, u32[]{:S(2)}) %collective-permute-start) | collective-permute-done | bytes 1048608 | tf_op jit(solution)/shard_map/ppermute | solution.py:19
  246.7 20.8 %collective-permute-done.1 = bf16[128,4096]{1,0:T(8,128)(2,1)S(1)} collective-permute-done((bf16[128,4096]{1,0:T(8,128)(2,1)}, bf16[128,4096]{1,0:T(8,128)(2,1)S(1)}, u32[]{:S(2)}, u32[]{:S(2)}) %collective-permute-start.1) | collective-permute-done | bytes 1048608 | tf_op jit(solution)/shard_map/ppermute | solution.py:22
  270.6 21.2 %collective-permute-done.2 = bf16[128,4096]{1,0:T(8,128)(2,1)} collective-permute-done((bf16[128,4096]{1,0:T(8,128)(2,1)S(1)}, bf16[128,4096]{1,0:T(8,128)(2,1)}, u32[]{:S(2)}, u32[]{:S(2)}) %collective-permute-start.2) | collective-permute-done | bytes 1048608 | tf_op jit(solution)/shard_map/ppermute | solution.py:19
  291.8 72.1 %collective-permute-done.3 = bf16[128,4096]{1,0:T(8,128)(2,1)} collective-permute-done((bf16[128,4096]{1,0:T(8,128)(2,1)S(1)}, bf16[128,4096]{1,0:T(8,128)(2,1)}, u32[]{:S(2)}, u32[]{:S(2)}) %collective-permute-start.3) | collective-permute-done | bytes 1048608 | tf_op jit(solution)/shard_map/ppermute | solution.py:22
  377.5 107.3 %all-gather.3 = bf16[16,1,128]{2,1,0:T(2,128)(2,1)S(1)} all-gather(bf16[1,1,128]{2,1,0:T(2,128)(2,1)S(1)} %bitcast.194), channel_id=1, replica_groups=mesh['dp'=4,'ctx'=4,'tp'=2] {'dp','ctx'}, dimensions={0}, use_global_device_ids=true | all-gather | bytes 4352 | tf_op jit(solution)/shard_map/all_gather | solution.py:132
  484.8 28.3 %all-gather.2 = bf16[16,1,128]{2,1,0:T(2,128)(2,1)S(1)} all-gather(bf16[1,1,128]{2,1,0:T(2,128)(2,1)S(1)} %bitcast.195), channel_id=1, replica_groups=mesh['dp'=4,'ctx'=4,'tp'=2] {'dp','ctx'}, dimensions={0}, use_global_device_ids=true | all-gather | bytes 4352 | tf_op jit(solution)/shard_map/all_gather | solution.py:131
  524.9 15.2 collective-permute-done.7
  547.1 15.6 collective-permute-done.8
  568.4 17.7 collective-permute-done.9
  590.8 16.7 collective-permute-done.10
  612.2 19.0 collective-permute-done.11
  635.8 16.8 collective-permute-done.12
  657.2 19.1 collective-permute-done.13
  677.3 20.1 collective-permute-done.14
  717.0 20.5 %fusion.81 = (bf16[512,4096]{1,0:T(8,128)(2,1)S(1)}, f32[512,4096]{1,0:T(8,128)}) fusion(f32[512,4096]{1,0:T(8,128)} %fusion.111, bf16[2048,4096]{1,0:T(8,128)(2,1)} %constant_dynamic-update-slice_fusion, bf16[512,2048]{1,0:T(8,128)(2,1)S(1)} %copy-done.6, bf16[512,2048]{1,0:T(8,128)(2,1)S(1)} %copy-done, f32[2048]{0:T(1024)S(1)} %bitcast.190, ...), kind=kOutput, calls=%fused_computation.119 | convolution fusion | flops 8640266240 | bytes 41963520 | tf_op jit(solution)/shard_map/dot_general | solution.py:140
  752.4 17.0 convolution_convert_fusion.3
  771.4 107.4 %all-reduce.15.cloned.1.call-done = (bf16[512,2048]{1,0:T(8,128)(2,1)}, bf16[512,2048]{1,0:T(8,128)(2,1)}) async-done(((bf16[512,2048]{1,0:T(8,128)(2,1)}, bf16[512,2048]{1,0:T(8,128)(2,1)}), (bf16[512,2048]{1,0:T(8,128)(2,1)}, bf16[512,2048]{1,0:T(8,128)(2,1)})) %all-reduce.15.cloned.1.call-update) | async-done | bytes 4194320 | tf_op jit(solution)/shard_map/psum | solution.py:143
  923.3 56.9 %reduce-scatter.7.cloned.1.call-done = bf16[512,256]{0,1:T(8,128)(2,1)} async-done(((bf16[2048,256]{0,1:T(8,128)(2,1)}), bf16[512,256]{0,1:T(8,128)(2,1)}) %reduce-scatter.7.cloned.1.call-update) | async-done | bytes 262160 | tf_op jit(solution)/shard_map/reduce_scatter | solution.py:220
  980.3 21.4 %convolution_bitcast_fusion.1 = f32[2048,4096]{0,1:T(8,128)} fusion(bf16[512,2048]{1,0:T(8,128)(2,1)} %param.27, f32[512,4096]{1,0:T(8,128)} %get-tuple-element.583), kind=kOutput, calls=%fused_computation.110 | convolution fusion | flops 8608808960 | bytes 44040192 | tf_op jit(solution)/shard_map/dot_general | solution.py:46
  1001.8 49.0 %all-reduce.13.cloned.1.call-done = (bf16[512,2048]{1,0:T(8,128)(2,1)}, bf16[512,256]{0,1:T(8,128)(2,1)}) async-done(((bf16[512,2048]{1,0:T(8,128)(2,1)}, bf16[512,256]{0,1:T(8,128)(2,1)}), (bf16[512,2048]{1,0:T(8,128)(2,1)}, bf16[512,256]{0,1:T(8,128)(2,1)})) %all-reduce.13.cloned.1.call-update) | async-done | bytes 2359312 | tf_op jit(solution)/shard_map/psum | solution.py:225
  1073.3 25.8 %fusion.106 = f32[2048,4096]{1,0:T(8,128)} fusion(bf16[512,4096]{1,0:T(8,128)(2,1)} %copy-done.39, bf16[512,2048]{1,0:T(8,128)(2,1)} %all-reduce.11.cloned.1.call-done, bf16[512,2048]{1,0:T(8,128)(2,1)S(1)} %copy-done, f32[2048]{0:T(1024)S(1)} %bitcast.191, f32[2048]{0:T(1024)S(1)} %bitcast.187, f32[512]{0:T(512)S(1)} %fusion.104, ...), kind=kOutput, calls=%fused_computation.199 | convolution fusion | flops 8598323200 | bytes 41963520 | tf_op jit(solution)/shard_map/dot_general | solution.py:46
  1110.4 66.2 %all-reduce.4 = (f32[2048]{0:T(1024)S(1)}, f32[2048]{0:T(1024)S(1)}, f32[2048]{0:T(1024)S(1)}, f32[2048]{0:T(1024)S(1)}, f32[3]{0:T(128)S(1)}) all-reduce(f32[2048]{0:T(1024)S(1)} %get-tuple-element.498, f32[2048]{0:T(1024)S(1)} %get-tuple-element.503, ...), channel_id=3, replica_groups=mesh['dp'=4,'ctx'=4,'tp'=2] {'dp','ctx'}, use_global_device_ids=true, to_apply=%region_24.25.clone | all-reduce | flops 8195 | bytes 65560
  1186.1 203.8 %reduce-scatter.17.cloned.1.call-done = f32[128,4096]{0,1:T(8,128)} async-done(((f32[2048,4096]{0,1:T(8,128)}), f32[128,4096]{0,1:T(8,128)}) %reduce-scatter.17.cloned.1.call-update) | async-done | bytes 2097168 | tf_op jit(solution)/shard_map/reduce_scatter | solution.py:173
  1392.8 62.1 %reduce-scatter.11.cloned.1.call-done = f32[128,256]{1,0:T(8,128)} async-done(((f32[2048,256]{1,0:T(8,128)}), f32[128,256]{1,0:T(8,128)}) %reduce-scatter.11.cloned.1.call-update) | async-done | bytes 131088 | tf_op jit(solution)/shard_map/reduce_scatter | solution.py:238
  1454.9 108.7 %reduce-scatter.9.cloned.1.call-done = f32[128,1024]{1,0:T(8,128)} async-done(((f32[2048,1024]{1,0:T(8,128)}), f32[128,1024]{1,0:T(8,128)}) %reduce-scatter.9.cloned.1.call-update) | async-done | bytes 524304 | tf_op jit(solution)/shard_map/reduce_scatter | solution.py:237
  1563.6 109.6 %reduce-scatter.13.cloned.1.call-done = f32[128,1024]{1,0:T(8,128)} async-done(((f32[2048,1024]{1,0:T(8,128)}), f32[128,1024]{1,0:T(8,128)}) %reduce-scatter.13.cloned.1.call-update) | async-done | bytes 524304 | tf_op jit(solution)/shard_map/reduce_scatter | solution.py:239
  1673.2 337.8 %reduce-scatter.15.cloned.1.call-done = f32[128,4096]{1,0:T(8,128)} async-done(((f32[2048,4096]{1,0:T(8,128)}), f32[128,4096]{1,0:T(8,128)}) %reduce-scatter.15.cloned.1.call-update) | async-done | bytes 2097168 | tf_op jit(solution)/shard_map/reduce_scatter | solution.py:172
  (222 shorter events, 256.7 us)
Async XLA Ops:
  7.2 70.6 %all-gather.10.cloned.1.call-start = ((), (), s32[]{:S(2)}) async-start(), calls=%async_computation.6 | async-start | bytes 1114112 | tf_op jit(solution)/shard_map/all_gather | solution.py:66
  7.9 100.2 %all-gather.12.cloned.1.call-start = ((), (), s32[]{:S(2)}) async-start(), calls=%async_computation.7 | async-start | bytes 1310720 | tf_op jit(solution)/shard_map/all_gather | solution.py:79
  81.1 79.5 %all-gather.14.cloned.1.call-start = ((), (), s32[]{:S(2)}) async-start(), calls=%async_computation.8 | async-start | bytes 4456448 | tf_op jit(solution)/shard_map/all_gather | solution.py:65
  81.9 129.9 %all-gather.16.cloned.1.call-start = ((), (), s32[]{:S(2)}) async-start(), calls=%async_computation.9 | async-start | bytes 4456448 | tf_op jit(solution)/shard_map/all_gather | solution.py:67
  82.4 616.2 %all-reduce.11.cloned.1.call-start = ((), (), s32[]{:S(2)}) async-start(), calls=%async_computation.10 | async-start | bytes 4194304 | tf_op jit(solution)/shard_map/psum | solution.py:126
  217.7 484.3 %all-gather.18.cloned.1.call-start = ((), (), s32[]{:S(2)}) async-start(), calls=%async_computation.11 | async-start | bytes 17825792 | tf_op jit(solution)/shard_map/all_gather | solution.py:134
  218.2 660.5 %all-reduce.15.cloned.1.call-start = ((), (), s32[]{:S(2)}) async-start(), calls=%async_computation.19 | async-start | bytes 8388608 | tf_op jit(solution)/shard_map/psum | solution.py:143
  218.3 28.4 %collective-permute-start = (bf16[128,4096]{1,0:T(8,128)(2,1)}, bf16[128,4096]{1,0:T(8,128)(2,1)S(1)}, u32[]{:S(2)}, u32[]{:S(2)}) collective-permute-start(bf16[128,4096]{1,0:T(8,128)(2,1)} %param.25), channel_id=1, source_target_pairs={{0,2},{2,4},{4,6},{6,8},{8,10},{10,12},{12,14},{14,16},{16,18},{18... | collective-permute-start | bytes 3145736 | tf_op jit(solution)/shard_map/ppermute | solution.py:19
  219.8 47.7 %collective-permute-start.1 = (bf16[128,4096]{1,0:T(8,128)(2,1)}, bf16[128,4096]{1,0:T(8,128)(2,1)S(1)}, u32[]{:S(2)}, u32[]{:S(2)}) collective-permute-start(bf16[128,4096]{1,0:T(8,128)(2,1)} %param.25), channel_id=1, source_target_pairs={{0,30},{2,0},{4,2},{6,4},{8,6},{10,8},{12,10},{14,12},{16,14},{18,... | collective-permute-start | bytes 3145736 | tf_op jit(solution)/shard_map/ppermute | solution.py:22
  246.7 117.2 %copy-start.18 = (bf16[128,4096]{1,0:T(8,128)(2,1)}, bf16[128,4096]{1,0:T(8,128)(2,1)S(1)}, u32[]{:S(2)}) copy-start(bf16[128,4096]{1,0:T(8,128)(2,1)S(1)} %collective-permute-done) | copy-start | bytes 3145732
  246.7 45.1 %collective-permute-start.2 = (bf16[128,4096]{1,0:T(8,128)(2,1)S(1)}, bf16[128,4096]{1,0:T(8,128)(2,1)}, u32[]{:S(2)}, u32[]{:S(2)}) collective-permute-start(bf16[128,4096]{1,0:T(8,128)(2,1)S(1)} %collective-permute-done), channel_id=1, source_target_pairs={{0,2},{2,4},{4,6},{6,8},{8,10},{10,12},{12,14},{14,16},{16,18},{18... | collective-permute-start | bytes 3145736 | tf_op jit(solution)/shard_map/ppermute | solution.py:19
  267.5 96.4 %collective-permute-start.3 = (bf16[128,4096]{1,0:T(8,128)(2,1)S(1)}, bf16[128,4096]{1,0:T(8,128)(2,1)}, u32[]{:S(2)}, u32[]{:S(2)}) collective-permute-start(bf16[128,4096]{1,0:T(8,128)(2,1)S(1)} %collective-permute-done.1), channel_id=1, source_target_pairs={{0,30},{2,0},{4,2},{6,4},{8,6},{10,8},{12,10},{14,12},{16,14},{18,... | collective-permute-start | bytes 3145736 | tf_op jit(solution)/shard_map/ppermute | solution.py:22
  291.8 78.6 %collective-permute-start.4 = (bf16[128,4096]{1,0:T(8,128)(2,1)}, bf16[128,4096]{1,0:T(8,128)(2,1)}, u32[]{:S(2)}, u32[]{:S(2)}) collective-permute-start(bf16[128,4096]{1,0:T(8,128)(2,1)} %collective-permute-done.2), channel_id=1, source_target_pairs={{0,2},{2,4},{4,6},{6,8},{8,10},{10,12},{12,14},{14,16},{16,18},{18... | collective-permute-start | bytes 3145736 | tf_op jit(solution)/shard_map/ppermute | solution.py:19
  363.9 151.6 %collective-permute-start.5 = (bf16[128,4096]{1,0:T(8,128)(2,1)}, bf16[128,4096]{1,0:T(8,128)(2,1)S(1)}, u32[]{:S(2)}, u32[]{:S(2)}) collective-permute-start(bf16[128,4096]{1,0:T(8,128)(2,1)} %collective-permute-done.3), channel_id=1, source_target_pairs={{0,30},{2,0},{4,2},{6,4},{8,6},{10,8},{12,10},{14,12},{16,14},{18,... | collective-permute-start | bytes 3145736 | tf_op jit(solution)/shard_map/ppermute | solution.py:22
  363.9 120.9 %copy-start.36 = (bf16[128]{0:T(256)(128)(2,1)S(1)}, bf16[128]{0:T(256)(128)(2,1)}, u32[]{:S(2)}) copy-start(bf16[128]{0:T(256)(128)(2,1)} %param.23) | copy-start | bytes 772
  370.4 148.4 %collective-permute-start.6 = (bf16[128,4096]{1,0:T(8,128)(2,1)}, bf16[128,4096]{1,0:T(8,128)(2,1)}, u32[]{:S(2)}, u32[]{:S(2)}) collective-permute-start(bf16[128,4096]{1,0:T(8,128)(2,1)} %collective-permute-done.4), channel_id=1, source_target_pairs={{0,2},{2,4},{4,6},{6,8},{8,10},{10,12},{12,14},{14,16},{16,18},{18... | collective-permute-start | bytes 3145736 | tf_op jit(solution)/shard_map/ppermute | solution.py:19
  484.8 232.3 %copy-start.33 = (f32[16,1,128]{2,1,0:T(1,128)}, f32[16,1,128]{2,1,0:T(1,128)S(1)}, u32[]{:S(2)}) copy-start(f32[16,1,128]{2,1,0:T(1,128)S(1)} %convert_element_type.139) | copy-start | bytes 24580
  515.5 24.6 %collective-permute-start.7 = (bf16[128,4096]{1,0:T(8,128)(2,1)S(1)}, bf16[128,4096]{1,0:T(8,128)(2,1)S(1)}, u32[]{:S(2)}, u32[]{:S(2)}) collective-permute-start(bf16[128,4096]{1,0:T(8,128)(2,1)S(1)} %collective-permute-done.5), channel_id=1, source_target_pairs={{0,30},{2,0},{4,2},{6,4},{8,6},{10,8},{12,10},{14,12},{16,14},{18,... | collective-permute-start | bytes 3145736 | tf_op jit(solution)/shard_map/ppermute | solution.py:22
  518.8 43.9 %collective-permute-start.8 = (bf16[128,4096]{1,0:T(8,128)(2,1)}, bf16[128,4096]{1,0:T(8,128)(2,1)S(1)}, u32[]{:S(2)}, u32[]{:S(2)}) collective-permute-start(bf16[128,4096]{1,0:T(8,128)(2,1)} %collective-permute-done.6), channel_id=1, source_target_pairs={{0,2},{2,4},{4,6},{6,8},{8,10},{10,12},{12,14},{14,16},{16,18},{18... | collective-permute-start | bytes 3145736 | tf_op jit(solution)/shard_map/ppermute | solution.py:19
  540.1 46.0 %collective-permute-start.9 = (bf16[128,4096]{1,0:T(8,128)(2,1)S(1)}, bf16[128,4096]{1,0:T(8,128)(2,1)S(1)}, u32[]{:S(2)}, u32[]{:S(2)}) collective-permute-start(bf16[128,4096]{1,0:T(8,128)(2,1)S(1)} %collective-permute-done.7), channel_id=1, source_target_pairs={{0,30},{2,0},{4,2},{6,4},{8,6},{10,8},{12,10},{14,12},{16,14},{18,... | collective-permute-start | bytes 3145736 | tf_op jit(solution)/shard_map/ppermute | solution.py:22
  562.7 44.9 %collective-permute-start.10 = (bf16[128,4096]{1,0:T(8,128)(2,1)S(1)}, bf16[128,4096]{1,0:T(8,128)(2,1)S(1)}, u32[]{:S(2)}, u32[]{:S(2)}) collective-permute-start(bf16[128,4096]{1,0:T(8,128)(2,1)S(1)} %collective-permute-done.8), channel_id=1, source_target_pairs={{0,2},{2,4},{4,6},{6,8},{8,10},{10,12},{12,14},{14,16},{16,18},{18... | collective-permute-start | bytes 3145736 | tf_op jit(solution)/shard_map/ppermute | solution.py:19
  586.2 45.0 %collective-permute-start.11 = (bf16[128,4096]{1,0:T(8,128)(2,1)S(1)}, bf16[128,4096]{1,0:T(8,128)(2,1)S(1)}, u32[]{:S(2)}, u32[]{:S(2)}) collective-permute-start(bf16[128,4096]{1,0:T(8,128)(2,1)S(1)} %collective-permute-done.9), channel_id=1, source_target_pairs={{0,30},{2,0},{4,2},{6,4},{8,6},{10,8},{12,10},{14,12},{16,14},{18,... | collective-permute-start | bytes 3145736 | tf_op jit(solution)/shard_map/ppermute | solution.py:22
  607.6 45.0 %collective-permute-start.12 = (bf16[128,4096]{1,0:T(8,128)(2,1)S(1)}, bf16[128,4096]{1,0:T(8,128)(2,1)S(1)}, u32[]{:S(2)}, u32[]{:S(2)}) collective-permute-start(bf16[128,4096]{1,0:T(8,128)(2,1)S(1)} %collective-permute-done.10), channel_id=1, source_target_pairs={{0,2},{2,4},{4,6},{6,8},{8,10},{10,12},{12,14},{14,16},{16,18},{18... | collective-permute-start | bytes 3145736 | tf_op jit(solution)/shard_map/ppermute | solution.py:19
  631.2 45.0 %collective-permute-start.13 = (bf16[128,4096]{1,0:T(8,128)(2,1)S(1)}, bf16[128,4096]{1,0:T(8,128)(2,1)S(1)}, u32[]{:S(2)}, u32[]{:S(2)}) collective-permute-start(bf16[128,4096]{1,0:T(8,128)(2,1)S(1)} %collective-permute-done.11), channel_id=1, source_target_pairs={{0,30},{2,0},{4,2},{6,4},{8,6},{10,8},{12,10},{14,12},{16,14},{18,... | collective-permute-start | bytes 3145736 | tf_op jit(solution)/shard_map/ppermute | solution.py:22
  652.6 44.9 %collective-permute-start.14 = (bf16[128,4096]{1,0:T(8,128)(2,1)S(1)}, bf16[128,4096]{1,0:T(8,128)(2,1)S(1)}, u32[]{:S(2)}, u32[]{:S(2)}) collective-permute-start(bf16[128,4096]{1,0:T(8,128)(2,1)S(1)} %collective-permute-done.12), channel_id=1, source_target_pairs={{0,2},{2,4},{4,6},{6,8},{8,10},{10,12},{12,14},{14,16},{16,18},{18... | collective-permute-start | bytes 3145736 | tf_op jit(solution)/shard_map/ppermute | solution.py:19
  769.5 210.7 %reduce-scatter.7.cloned.1.call-start = ((), (), s32[]{:S(2)}) async-start(), calls=%async_computation.12 | async-start | bytes 1310720 | tf_op jit(solution)/shard_map/reduce_scatter | solution.py:220
  915.5 135.3 %all-reduce.13.cloned.1.call-start = ((), (), s32[]{:S(2)}) async-start(), calls=%async_computation.18 | async-start | bytes 4718592 | tf_op jit(solution)/shard_map/psum | solution.py:225
  980.3 409.7 %reduce-scatter.17.cloned.1.call-start = ((), (), s32[]{:S(2)}) async-start(), calls=%async_computation.17 | async-start | bytes 35651584 | tf_op jit(solution)/shard_map/reduce_scatter | solution.py:173
  1001.7 453.2 %reduce-scatter.11.cloned.1.call-start = ((), (), s32[]{:S(2)}) async-start(), calls=%async_computation.14 | async-start | bytes 2228224 | tf_op jit(solution)/shard_map/reduce_scatter | solution.py:238
  1054.5 509.1 %reduce-scatter.9.cloned.1.call-start = ((), (), s32[]{:S(2)}) async-start(), calls=%async_computation.13 | async-start | bytes 8912896 | tf_op jit(solution)/shard_map/reduce_scatter | solution.py:237
  1062.2 611.0 %reduce-scatter.13.cloned.1.call-start = ((), (), s32[]{:S(2)}) async-start(), calls=%async_computation.15 | async-start | bytes 8912896 | tf_op jit(solution)/shard_map/reduce_scatter | solution.py:239
  1072.6 938.4 %reduce-scatter.15.cloned.1.call-start = ((), (), s32[]{:S(2)}) async-start(), calls=%async_computation.16 | async-start | bytes 35651584 | tf_op jit(solution)/shard_map/reduce_scatter | solution.py:172
  (37 other events, 349.0 us)
Sparse Core Ops, SparseCore 0:
  10.2 40.6 all-gather.9
  81.2 26.8 all-gather.11
  110.3 50.1 all-gather.13
  162.7 49.0 all-gather.15
  217.8 62.2 all-reduce.10
  282.4 202.0 all-gather.17
  769.6 109.0 all-reduce.14
  915.6 64.5 reduce-scatter.6
  983.3 67.4 all-reduce.12
  1054.9 334.9 reduce-scatter.16
  1394.2 60.6 reduce-scatter.10
  1460.0 103.6 reduce-scatter.8
  1568.8 104.3 reduce-scatter.12
  1678.5 332.4 reduce-scatter.14
